TPU v7x, 256 devices: a whole 4x4x8 slice. The times are simulated.
256 devices in a mesh: region: 32 (over y, z), sub: 8 (over x, core).
Axes of the slice: x: 4, y: 4, z: 8, core: 2. Of those that a mesh axis runs over, the one named last changes fastest.
Arguments:
- mode_rows: bfloat16 [131072, 4096], P(('region', 'sub')), may hold values from -0.09375 to 0.09375
- input_rows: bfloat16 [512, 4096], P(('region', 'sub')), may hold values from -0.25 to 0.25
- input_factor: bfloat16 [512, 128], P(('region', 'sub')), may hold values from -6 to 6
- mode_freq: float32 [4096], replicated, may hold values from 0.5 to 2
- mode_damping: float32 [4096], replicated, may hold values from 0.02 to 0.2
- line_freq: float32 [2], replicated, may hold values from 0.6 to 1.6
- boundary_rows: int32 [32768], P(('region', 'sub')), may hold values from 0 to 511
- connectivity: int32 [4, 131072], P(None, ('region', 'sub')), may hold values from 0 to 639
- stress_coef: float32 [4, 131072], P(None, ('region', 'sub')), may hold values from -3 to 3
Outputs:
- stress_psd: float32 [2, 131072], P(None, ('region', 'sub'))
Inputs may be any that keep to these rules, and one draw needn't show every extreme that they name: `boundary_rows`: local row numbers of the sending device. `connectivity`: rows of the node table of the element's device.
All inputs are finite; a program needn't handle non-finite values.
Results may differ from a plain program's by a relative error of at most 0.0013.
Values may be sent and summed in bfloat16 or wider, within the bound.
A program may use at most 64 MiB of HBM per device.

v0:
```python
import jax
import jax.numpy as jnp
from jax import lax
from jax.sharding import PartitionSpec as P


def extended(cells, sides, width):
    for axis, dim in sides:
        count = lax.axis_size(axis)
        ends = count - 1
        head = lax.slice_in_dim(cells, 0, width, axis=dim)
        tail = lax.slice_in_dim(cells, cells.shape[dim] - width, cells.shape[dim], axis=dim)
        cells = jnp.concatenate(
            [
                lax.ppermute(tail, axis, [(i, (i + 1) % count) for i in range(ends)]),
                cells,
                lax.ppermute(head, axis, [((i + 1) % count, i) for i in range(ends)]),
            ],
            axis=dim,
        )
    return cells


def modal_gain(mode_freq, mode_damping, line_omega):
    detune = mode_freq * mode_freq - line_omega * line_omega
    damped = 2.0 * mode_damping * mode_freq * line_omega
    magnitude = detune * detune + damped * damped
    return (detune / magnitude, -damped / magnitude)


def apply_gain(summed, gain_real, gain_imag):
    half_cols = summed.shape[1] // 2
    forced_real = summed[:, :half_cols]
    forced_imag = summed[:, half_cols:]
    out_real = gain_real[:, None] * forced_real - gain_imag[:, None] * forced_imag
    out_imag = gain_real[:, None] * forced_imag + gain_imag[:, None] * forced_real
    return jnp.concatenate([out_real, out_imag], axis=1).astype(jnp.bfloat16)


def scale_lines(summed, mode_freq, mode_damping, line_freq, columns):
    pieces = []
    for line_no in range(line_freq.shape[0]):
        gain_real, gain_imag = modal_gain(mode_freq, mode_damping, line_freq[line_no])
        pieces.append(
            apply_gain(summed[:, line_no * columns : (line_no + 1) * columns], gain_real, gain_imag)
        )
    return jnp.concatenate(pieces, axis=1)


def local(
    mode_rows,
    input_rows,
    input_factor,
    mode_freq,
    mode_damping,
    line_freq,
    boundary_rows,
    connectivity,
    stress_coef,
):
    mode_count = input_rows.shape[1]
    line_count = line_freq.shape[0]
    width_all = input_factor.shape[1]
    columns = width_all // line_count
    partial_value = lax.dot_general(
        input_rows, input_factor, (((0,), (0,)), ((), ())), preferred_element_type=jnp.float32
    )
    summed = lax.psum(
        partial_value.reshape(mode_count // 2, 2 * width_all), ("region", "sub")
    ).reshape(mode_count, width_all)
    pseudo = scale_lines(summed, mode_freq, mode_damping, line_freq, columns)
    responses = jnp.dot(mode_rows, pseudo, preferred_element_type=jnp.float32).astype(jnp.bfloat16)
    rim_rows = boundary_rows.shape[0] // 2
    export = responses[boundary_rows]
    padded = extended(export, ((("region", "sub"), 0),), rim_rows)
    node_table = jnp.concatenate([padded[:rim_rows], responses, padded[3 * rim_rows :]], axis=0)
    stress = stress_coef[0][:, None] * node_table[connectivity[0]].astype(jnp.float32)
    for corner in range(1, connectivity.shape[0]):
        stress = stress + stress_coef[corner][:, None] * node_table[connectivity[corner]].astype(
            jnp.float32
        )
    squares = stress * stress
    power = jnp.stack(
        [
            jnp.mean(squares[:, line_no * columns : (line_no + 1) * columns], axis=1)
            for line_no in range(line_count)
        ],
        axis=0,
    )
    return power


def solution(mesh):
    placed = (
        P(("region", "sub"), None),
        P(("region", "sub"), None),
        P(("region", "sub"), None),
        P(),
        P(),
        P(),
        P(("region", "sub")),
        P(None, ("region", "sub")),
        P(None, ("region", "sub")),
    )
    return jax.shard_map(
        local, mesh=mesh, in_specs=placed, out_specs=P(None, ("region", "sub")), check_vma=False
    )
```

profile of v0, /device:TPU:24, one launch (start us, length us, event | category | flops | bytes accessed | tf_op | source)
XLA Modules:
  0.0 312.2 jit_solution(9872141562445316333)
XLA Ops:
  6.6 0.0 all-reduce.2.cloned.1.call-start
  6.6 0.6 copy-done
  7.3 2.4 fusion.14
  9.7 0.6 fusion.13
  12.9 1.2 fusion.9
  14.2 262.5 %all-reduce.2.cloned.1.call-done = f32[4096,128]{0,1:T(8,128)} async-done(((f32[4096,128]{0,1:T(8,128)}), f32[4096,128]{0,1:T(8,128)}) %all-reduce.2.cloned.1.call-update) | async-done | bytes 2097168 | tf_op jit(solution)/shard_map/psum | solution.py:68
  276.7 1.8 subtract_convert_fusion.1
  278.5 3.7 %fusion = bf16[512,128]{0,1:T(8,128)(2,1)S(1)} fusion(bf16[512,4096]{1,0:T(8,128)(2,1)} %param.9, bf16[4096,32]{0,1:T(8,128)(2,1)S(1)} %get-tuple-element.11, bf16[4096,32]{0,1:T(8,128)(2,1)S(1)} %get-tuple-element.12, bf16[4096,32]{0,1:T(8,128)(2,1)S(1)} %get-tuple-element.8, bf16[4096,32]{0,1:T(8,128)(2,1)S(1)} %get-tuple-element.7), kind=kOutput, calls=%fused_computation.6 | convolution fusion | flops 541130752 | bytes 5373952 | tf_op jit(solution)/shard_map/dot_general | solution.py:72
  282.2 0.1 copy.25
  282.3 0.7 gather_fusion
  283.0 0.1 copy.34
  283.1 5.7 %collective-permute-start.1 = (bf16[64,128]{0,1:T(8,128)(2,1)S(1)}, bf16[64,128]{0,1:T(8,128)(2,1)S(1)}, u32[]{:S(2)}, u32[]{:S(2)}) collective-permute-start(bf16[64,128]{0,1:T(8,128)(2,1)S(1)} %copy.34), channel_id=1, source_target_pairs={{1,0},{2,1},{3,2},{4,3},{5,4},{6,5},{7,6},{8,7},{9,8},{10,9},{11,1... | collective-permute-start | bytes 49160 | tf_op jit(solution)/shard_map/ppermute | solution.py:17
  288.8 0.1 copy.33
  289.0 1.9 collective-permute-start
  290.9 7.5 %collective-permute-done = bf16[64,128]{0,1:T(8,128)(2,1)S(1)} collective-permute-done((bf16[64,128]{0,1:T(8,128)(2,1)S(1)}, bf16[64,128]{0,1:T(8,128)(2,1)S(1)}, u32[]{:S(2)}, u32[]{:S(2)}) %collective-permute-start) | collective-permute-done | bytes 16416 | tf_op jit(solution)/shard_map/ppermute | solution.py:15
  298.4 0.1 pad_maximum_fusion
  298.5 0.2 copy.28
  298.7 1.3 gather_fusion.4
  300.1 1.3 gather_fusion.3
  301.4 1.3 gather_fusion.2
  302.7 1.3 gather_fusion.1
  304.1 0.3 add_multiply_fusion
  304.4 0.3 slice_reduce_fusion.1
  304.8 0.6 pad_maximum_fusion.1
  (25 shorter events, 0.1 us)
Async XLA Ops:
  6.5 0.7 copy-start
  6.5 3.2 %copy-start.5 = (f32[2]{0:T(128)S(1)}, f32[2]{0:T(128)}, u32[]{:S(2)}) copy-start(f32[2]{0:T(128)} %param.14) | copy-start | bytes 28
  6.5 3.8 %copy-start.6 = (s32[128]{0:T(128)S(1)}, s32[128]{0:T(128)}, u32[]{:S(2)}) copy-start(s32[128]{0:T(128)} %param.15) | copy-start | bytes 1540
  6.5 6.2 %copy-start.3 = (s32[4,512]{1,0:T(4,128)S(1)}, s32[4,512]{1,0:T(4,128)}, u32[]{:S(2)}) copy-start(s32[4,512]{1,0:T(4,128)} %param.16) | copy-start | bytes 24580
  6.5 6.3 %copy-start.4 = (f32[4,512]{1,0:T(4,128)S(1)}, f32[4,512]{1,0:T(4,128)}, u32[]{:S(2)}) copy-start(f32[4,512]{1,0:T(4,128)} %param.17) | copy-start | bytes 24580
  6.5 6.3 %copy-start.1 = (f32[4096]{0:T(1024)S(1)}, f32[4096]{0:T(1024)}, u32[]{:S(2)}) copy-start(f32[4096]{0:T(1024)} %param.12) | copy-start | bytes 49156
  6.6 6.3 %copy-start.2 = (f32[4096]{0:T(1024)S(1)}, f32[4096]{0:T(1024)}, u32[]{:S(2)}) copy-start(f32[4096]{0:T(1024)} %param.13) | copy-start | bytes 49156
  6.6 270.1 %all-reduce.2.cloned.1.call-start = ((), (), s32[]{:S(2)}) async-start(), calls=%async_computation | async-start | bytes 4194304 | tf_op jit(solution)/shard_map/psum | solution.py:68
  283.1 7.8 %collective-permute-start.1 = (bf16[64,128]{0,1:T(8,128)(2,1)S(1)}, bf16[64,128]{0,1:T(8,128)(2,1)S(1)}, u32[]{:S(2)}, u32[]{:S(2)}) collective-permute-start(bf16[64,128]{0,1:T(8,128)(2,1)S(1)} %copy.34), channel_id=1, source_target_pairs={{1,0},{2,1},{3,2},{4,3},{5,4},{6,5},{7,6},{8,7},{9,8},{10,9},{11,1... | collective-permute-start | bytes 49160 | tf_op jit(solution)/shard_map/ppermute | solution.py:17
  289.0 9.5 %collective-permute-start = (bf16[64,128]{0,1:T(8,128)(2,1)S(1)}, bf16[64,128]{0,1:T(8,128)(2,1)S(1)}, u32[]{:S(2)}, u32[]{:S(2)}) collective-permute-start(bf16[64,128]{0,1:T(8,128)(2,1)S(1)} %copy.33), channel_id=1, source_target_pairs={{0,1},{1,2},{2,3},{3,4},{4,5},{5,6},{6,7},{7,8},{8,9},{9,10},{10,1... | collective-permute-start | bytes 49160 | tf_op jit(solution)/shard_map/ppermute | solution.py:15
Sparse Core Ops, SparseCore 0:
  12.8 263.8 all-reduce.1
where the time goes:
time: 313 us; the launch traced here: 312 us
  waiting for transfers between devices  270 us (86%)
  between operations  16.1 us (5%)
  local copies, waits for them, and re-layouts  7.86 us (3%)
  starting transfers between devices  7.65 us (2%)
  matrix products  6.16 us (2%)
  other arithmetic  4.44 us (1%)
    psum x1, waiting for transfers between devices, local(): lax.psum(partial_value.reshape(mode_count // 2, 2 * width_all), ('region'...  263 us
    ppermute x1, waiting for transfers between devices, extended(): lax.ppermute(tail, axis, [(i, (i + 1) % count) for i in range(ends)])  7.5 us
  transfers between devices with their start and end apart: 3, of which 2 were waited for; matrix products, arithmetic and copies ran while one was open for 1% of the time, Pallas kernels for 0%

commit v1 on v0

--- a/solution.py
+++ b/solution.py
@@ -66,7 +66,7 @@
         input_rows, input_factor, (((0,), (0,)), ((), ())), preferred_element_type=jnp.float32
     )
     summed = lax.psum(
-        partial_value.reshape(mode_count // 2, 2 * width_all), ("region", "sub")
+        lax.psum(partial_value.reshape(mode_count // 2, 2 * width_all), "region"), "sub"
     ).reshape(mode_count, width_all)
     pseudo = scale_lines(summed, mode_freq, mode_damping, line_freq, columns)
     responses = jnp.dot(mode_rows, pseudo, preferred_element_type=jnp.float32).astype(jnp.bfloat16)

time: 313 us -> 276 us (0.88)
  waiting for transfers between devices: 270 us -> 228 us
  local copies, waits for them, and re-layouts: 7.86 us -> 13.6 us
    psum x1 -> x2, waiting for transfers between devices: 263 us -> 221 us  [the longest x1 155 us: local(): lax.psum(partial_value.reshape(mode_count // 2, 2 * width_all), 'region')]
    reshape x0 -> x3, local copies, waits for them, and re-layouts: none -> 5.12 us  [the longest x2 3.49 us: local(): summed = lax.psum(lax.psum(partial_value.reshape(mode_count // 2, 2 * wid...]
  transfers between devices with their start and end apart: 3 -> 4, of which waited for: 2 -> 3; matrix products, arithmetic and copies ran while one was open for 1% -> 1% of each run, Pallas kernels for 0% -> 0%
where the time goes in v1:
time: 276 us; the launch traced here: 275 us
  waiting for transfers between devices  228 us (83%)
  between operations  16.1 us (6%)
  local copies, waits for them, and re-layouts  13.6 us (5%)
  starting transfers between devices  8.15 us (3%)
  matrix products  4.9 us (2%)
  other arithmetic  4.43 us (2%)
    psum x1, waiting for transfers between devices, local(): lax.psum(partial_value.reshape(mode_count // 2, 2 * width_all), 'region')  155 us
    psum x1, waiting for transfers between devices, local(): lax.psum(lax.psum(partial_value.reshape(mode_count // 2, 2 * width_all),...  65.9 us
    ppermute x1, waiting for transfers between devices, extended(): lax.ppermute(tail, axis, [(i, (i + 1) % count) for i in range(ends)])  7.5 us
    ppermute x1, starting transfers between devices, extended(): lax.ppermute(head, axis, [((i + 1) % count, i) for i in range(ends)])  6.19 us
  transfers between devices with their start and end apart: 4, of which 3 were waited for; matrix products, arithmetic and copies ran while one was open for 1% of the time, Pallas kernels for 0%

profile of v1, /device:TPU:24, one launch (start us, length us, event | category | flops | bytes accessed | tf_op | source)
XLA Modules:
  0.0 275.3 jit_solution(2801340706386277494)
XLA Ops:
  6.5 0.7 copy-done
  7.3 1.2 fusion.14
  8.4 1.6 reshape.144
  10.1 0.6 copy-done.5
  10.7 0.6 fusion.13
  11.3 154.6 %all-reduce.3.cloned.1.call-done = f32[2048,256]{1,0:T(8,128)} async-done(((f32[2048,256]{1,0:T(8,128)}), f32[2048,256]{1,0:T(8,128)}) %all-reduce.3.cloned.1.call-update) | async-done | bytes 2097168 | tf_op jit(solution)/shard_map/psum | solution.py:69
  166.0 1.6 reshape.145
  167.6 1.9 copy.31
  172.1 1.2 fusion.9
  173.3 65.9 %all-reduce.5.cloned.1.call-done = f32[4096,128]{0,1:T(8,128)} async-done(((f32[4096,128]{0,1:T(8,128)}), f32[4096,128]{0,1:T(8,128)}) %all-reduce.5.cloned.1.call-update) | async-done | bytes 2097168 | tf_op jit(solution)/shard_map/psum | solution.py:68
  239.3 1.8 subtract_convert_fusion.1
  241.1 3.7 %fusion = bf16[512,128]{0,1:T(8,128)(2,1)S(1)} fusion(bf16[512,4096]{1,0:T(8,128)(2,1)} %param.9, bf16[4096,32]{0,1:T(8,128)(2,1)S(1)} %get-tuple-element.11, bf16[4096,32]{0,1:T(8,128)(2,1)S(1)} %get-tuple-element.12, bf16[4096,32]{0,1:T(8,128)(2,1)S(1)} %get-tuple-element.8, bf16[4096,32]{0,1:T(8,128)(2,1)S(1)} %get-tuple-element.7), kind=kOutput, calls=%fused_computation.6 | convolution fusion | flops 541130752 | bytes 5373952 | tf_op jit(solution)/shard_map/dot_general | solution.py:72
  244.9 0.7 gather_fusion
  245.7 6.2 %collective-permute-start.1 = (bf16[64,128]{0,1:T(8,128)(2,1)S(1)}, bf16[64,128]{0,1:T(8,128)(2,1)S(1)}, u32[]{:S(2)}, u32[]{:S(2)}) collective-permute-start(bf16[64,128]{0,1:T(8,128)(2,1)S(1)} %copy.40), channel_id=1, source_target_pairs={{1,0},{2,1},{3,2},{4,3},{5,4},{6,5},{7,6},{8,7},{9,8},{10,9},{11,1... | collective-permute-start | bytes 49160 | tf_op jit(solution)/shard_map/ppermute | solution.py:17
  252.1 1.9 collective-permute-start
  254.0 7.5 %collective-permute-done = bf16[64,128]{0,1:T(8,128)(2,1)S(1)} collective-permute-done((bf16[64,128]{0,1:T(8,128)(2,1)S(1)}, bf16[64,128]{0,1:T(8,128)(2,1)S(1)}, u32[]{:S(2)}, u32[]{:S(2)}) %collective-permute-start) | collective-permute-done | bytes 16416 | tf_op jit(solution)/shard_map/ppermute | solution.py:15
  261.6 0.2 copy.35
  261.8 1.3 gather_fusion.4
  263.1 1.3 gather_fusion.3
  264.5 1.3 gather_fusion.2
  265.8 1.3 gather_fusion.1
  267.2 0.3 add_multiply_fusion
  267.5 0.3 slice_reduce_fusion.1
  267.9 0.6 pad_maximum_fusion.1
  (31 shorter events, 0.6 us)
Async XLA Ops:
  6.5 0.7 copy-start
  6.5 159.4 %all-reduce.3.cloned.1.call-start = ((), (), s32[]{:S(2)}) async-start(), calls=%async_computation | async-start | bytes 4194304 | tf_op jit(solution)/shard_map/psum | solution.py:69
  10.1 0.7 copy-start.5
  10.1 1.2 copy-start.6
  10.1 229.2 %all-reduce.5.cloned.1.call-start = ((), (), s32[]{:S(2)}) async-start(), calls=%async_computation.1 | async-start | bytes 4194304 | tf_op jit(solution)/shard_map/psum | solution.py:68
  169.5 2.5 copy-start.3
  169.5 2.6 copy-start.4
  169.5 2.6 copy-start.1
  169.5 2.6 copy-start.2
  245.7 8.3 %collective-permute-start.1 = (bf16[64,128]{0,1:T(8,128)(2,1)S(1)}, bf16[64,128]{0,1:T(8,128)(2,1)S(1)}, u32[]{:S(2)}, u32[]{:S(2)}) collective-permute-start(bf16[64,128]{0,1:T(8,128)(2,1)S(1)} %copy.40), channel_id=1, source_target_pairs={{1,0},{2,1},{3,2},{4,3},{5,4},{6,5},{7,6},{8,7},{9,8},{10,9},{11,1... | collective-permute-start | bytes 49160 | tf_op jit(solution)/shard_map/ppermute | solution.py:17
  252.1 9.5 %collective-permute-start = (bf16[64,128]{0,1:T(8,128)(2,1)S(1)}, bf16[64,128]{0,1:T(8,128)(2,1)S(1)}, u32[]{:S(2)}, u32[]{:S(2)}) collective-permute-start(bf16[64,128]{0,1:T(8,128)(2,1)S(1)} %copy.39), channel_id=1, source_target_pairs={{0,1},{1,2},{2,3},{3,4},{4,5},{5,6},{6,7},{7,8},{8,9},{9,10},{10,1... | collective-permute-start | bytes 49160 | tf_op jit(solution)/shard_map/ppermute | solution.py:15
Sparse Core Ops, SparseCore 0:
  10.9 155.0 all-reduce.2
  169.6 69.6 all-reduce.4
